TPU v7x, 32 devices: a whole 2x2x4 slice. The times are simulated.
32 devices in a mesh: sample: 4 (over z), row: 2 (over y), col: 4 (over x, core).
Axes of the slice: x: 2, y: 2, z: 4, core: 2. Of those that a mesh axis runs over, the one named last changes fastest.
Arguments:
- single: bfloat16 [2048, 384], P(('sample', 'row')), parts along dimension 0, may hold values from -16 to 16
- pair_bias: bfloat16 [64, 512, 512], P('sample', 'row', 'col'), parts along dimension 0, may hold values from -4 to 400
- token_mask: int32 [2048], P('sample'), parts along dimension 0, may hold values from 0 to 1, as said below
- norm_gain: float32 [384], replicated, may hold values from 0.25 to 1.75
- w_query: bfloat16 [384, 384], replicated, may hold values from -0.3125 to 0.3125
- query_bias: float32 [384], replicated, may hold values from -3 to 3
- w_key: bfloat16 [384, 384], replicated, may hold values from -0.3125 to 0.3125
- w_value: bfloat16 [384, 384], replicated, may hold values from -0.3125 to 0.3125
- w_gate: bfloat16 [384, 384], replicated, may hold values from -0.3125 to 0.3125
- w_out: bfloat16 [384, 384], P(None, 'col'), may hold values from -0.3125 to 0.3125
Outputs:
- updated: float32 [2048, 384], P(('sample', 'row'), 'col'), parts along dimension 0
There are 4 independent parts, one for each index of `sample`. A program takes and returns all parts, laid end to end along the dimension named above; an argument that names none is the same for every part. Nothing has to cross between parts.
Inputs may be any that keep to these rules, and one draw needn't show every extreme that they name: `token_mask`: 1 for a leading run of 64 or more tokens and 0 for every token after it.
All inputs are finite; a program needn't handle non-finite values.
Results may differ from a plain program's by a relative error of at most 0.0014.
Values may be sent and summed in bfloat16 or wider, within the bound.
No kernel may reach another device: no remote copies, remote signals or barrier semaphores. Data moves between devices by JAX's collectives and lax.ppermute only.
A program may use at most 128 MiB of HBM per device.

v0:
```python
import math
import jax
import jax.numpy as jnp
from jax import lax
from jax.sharding import PartitionSpec as P

D = 384
HEADS = 16


def layer_norm(single, norm_gain):
    values_f32 = single.astype(jnp.float32)
    row_mean = jnp.mean(values_f32, axis=1, keepdims=True)
    centered = values_f32 - row_mean
    row_var = jnp.mean(centered * centered, axis=1, keepdims=True)
    return (centered * lax.rsqrt(row_var + 1e-05) * norm_gain).astype(jnp.bfloat16)


def attend(query_rows, key_rows, value_rows, bias_block, mask_cols):
    row_count = query_rows.shape[0]
    col_count = key_rows.shape[0]
    query_heads = query_rows.reshape(row_count, HEADS, -1)
    key_heads = key_rows.reshape(col_count, HEADS, -1)
    value_heads = value_rows.reshape(col_count, HEADS, -1)
    logits = jnp.einsum("qhd,khd->hqk", query_heads, key_heads, preferred_element_type=jnp.float32)
    mask_term = (mask_cols.astype(jnp.float32) - 1.0) * 1000000.0
    logits = logits + bias_block.astype(jnp.float32) + mask_term[None, None, :]
    row_peak = jnp.max(logits, axis=2)
    exp_scores = jnp.exp(logits - row_peak[:, :, None])
    row_total = jnp.sum(exp_scores, axis=2)
    weighted = jnp.einsum(
        "hqk,khd->qhd",
        exp_scores.astype(jnp.bfloat16),
        value_heads,
        preferred_element_type=jnp.float32,
    )
    return (row_peak.T, row_total.T, weighted.reshape(row_count, -1))


def on_device(
    single, pair_bias, token_mask, norm_gain, w_query, query_bias, w_key, w_value, w_gate, w_out
):
    head_dim = D // HEADS
    inv_sqrt = 1.0 / math.sqrt(head_dim)
    tok_rows = single.shape[0]
    col_total = lax.axis_size("col")
    out_width = w_out.shape[1]
    col_pos = lax.axis_index("col")
    normed = layer_norm(single, norm_gain)
    query = (
        (jnp.dot(normed, w_query, preferred_element_type=jnp.float32) + query_bias) * inv_sqrt
    ).astype(jnp.bfloat16)
    gate_act = jax.nn.sigmoid(jnp.dot(normed, w_gate, preferred_element_type=jnp.float32))
    single_cols = lax.dynamic_slice_in_dim(single, col_pos * out_width, out_width, 1).astype(
        jnp.float32
    )
    key_local = jnp.dot(normed, w_key, preferred_element_type=jnp.float32).astype(jnp.bfloat16)
    value_local = jnp.dot(normed, w_value, preferred_element_type=jnp.float32).astype(jnp.bfloat16)
    key_all, value_all = (
        lax.all_gather(key_local, "row", axis=0, tiled=True),
        lax.all_gather(value_local, "row", axis=0, tiled=True),
    )
    sub_rows = tok_rows // col_total
    query_start = col_pos * sub_rows
    bias_panel = lax.all_to_all(pair_bias, "col", split_axis=1, concat_axis=2, tiled=True)
    key_rows, value_rows = (key_all, value_all)
    query_part = lax.dynamic_slice_in_dim(query, query_start, sub_rows, 0)
    gate_part = lax.dynamic_slice_in_dim(gate_act, query_start, sub_rows, 0)
    row_peak, row_total, weighted = attend(query_part, key_rows, value_rows, bias_panel, token_mask)
    attended = weighted / jnp.repeat(row_total, head_dim, axis=1)
    gated_part = (gate_part * attended).astype(jnp.bfloat16)
    gated_all = lax.all_gather(gated_part, "col", axis=0, tiled=True)
    result = single_cols + jnp.dot(gated_all, w_out, preferred_element_type=jnp.float32)
    return result


def solution(mesh):
    return jax.shard_map(
        on_device,
        mesh=mesh,
        in_specs=(
            P(("sample", "row"), None),
            P("sample", "row", "col"),
            P("sample"),
            P(),
            P(),
            P(),
            P(),
            P(),
            P(),
            P(None, "col"),
        ),
        out_specs=P(("sample", "row"), "col"),
        check_vma=False,
    )
```

profile of v0, /device:TPU:0, one launch (start us, length us, event | category | flops | bytes accessed | tf_op | source)
XLA Modules:
  0.0 40.1 jit_solution(15966717443112249602)
XLA Ops:
  0.0 0.0 copy-start
  0.0 0.0 copy-start.1
  0.0 0.0 copy-start.5
  0.0 2.9 %copy.31 = bf16[16,256,128]{2,0,1:T(8,128)(2,1)} copy(bf16[16,256,128]{2,1,0:T(8,128)(2,1)} %param.11) | data formatting | bytes 2097152 | tf_op args[1]
  3.0 0.0 copy-start.2
  3.0 0.0 copy-start.8
  3.0 0.0 copy-start.6
  3.0 4.4 %all-to-all-start = ((bf16[16,256,128]{2,0,1:T(8,128)(2,1)}), bf16[16,256,128]{2,0,1:T(8,128)(2,1)S(1)}, u32[]{:S(2)}, u32[]{:S(2)}) async-start(bf16[16,256,128]{2,0,1:T(8,128)(2,1)} %copy.31), calls=%async_computation | async-start | bytes 2097152 | tf_op jit(solution)/shard_map/all_to_all | solution.py:65
  7.3 0.0 copy-done.1
  7.3 0.1 convert_reduce_fusion
  7.5 0.2 fusion.7
  7.7 0.0 copy-done
  7.7 0.0 copy-done.5
  7.7 0.3 convolution_convert_fusion.1
  8.0 0.0 copy-done.2
  8.0 0.3 fusion.18
  8.4 0.0 copy-start.7
  8.4 0.0 copy-start.3
  8.4 0.0 copy-done.8
  8.4 0.3 convolution_convert_fusion
  8.8 0.0 copy-done.6
  8.8 8.5 %all_gather.9 = bf16[512,384]{1,0:T(8,128)(2,1)S(1)} all-gather(bf16[256,384]{1,0:T(8,128)(2,1)S(1)} %convolution_convert_fusion.1), channel_id=1, replica_groups=mesh['sample'=4,'row'=2,'col'=4] {'row'}, dimensions={0}, use_global_device_ids=true | all-gather | bytes 589824 | tf_op jit(solution)/shard_map/all_gather | solution.py:61
  17.3 0.2 copy.28
  17.5 0.1 copy.29
  17.6 7.3 %all_gather.10 = bf16[512,384]{1,0:T(8,128)(2,1)S(1)} all-gather(bf16[256,384]{1,0:T(8,128)(2,1)S(1)} %convolution_convert_fusion), channel_id=1, replica_groups=mesh['sample'=4,'row'=2,'col'=4] {'row'}, dimensions={0}, use_global_device_ids=true | all-gather | bytes 589824 | tf_op jit(solution)/shard_map/all_gather | solution.py:60
  24.9 0.2 copy.30
  25.1 0.1 constant_dynamic-slice_fusion
  25.3 0.1 copy.34
  25.4 0.0 copy-done.7
  25.4 0.0 copy-done.3
  25.4 1.1 %fusion.21 = f32[256,384]{1,0:T(8,128)} fusion(bf16[384,384]{1,0:T(8,128)(2,1)S(1)} %copy-done.3, bf16[256,384]{1,0:T(8,128)(2,1)S(1)} %copy-done.1, f32[384]{0:T(512)S(1)} %copy-done.5, f32[256]{0:T(256)S(1)} %add_rsqrt_fusion, f32[256]{0:T(256)S(1)} %broadcast_multiply_fusion), kind=kOutput, calls=%fused_computation.32 | convolution fusion | flops 75988992 | bytes 888320 | tf_op jit(solution)/shard_map/dot_general | solution.py:53
  26.5 0.0 all-to-all-done
  26.5 2.2 %copy.36 = f32[16,4,64,128]{3,1,2,0:T(4,128)} copy(bf16[16,4,64,128]{3,0,2,1:T(8,128)(2,1)S(1)} %bitcast.24) | data formatting | bytes 3145728 | tf_op jit(solution)/shard_map/convert_element_type | solution.py:27
  28.6 2.1 %reshape.37 = f32[16,64,512]{2,1,0:T(8,128)S(1)} reshape(f32[16,64,4,128]{3,2,1,0:T(4,128)} %bitcast.23) | data formatting | bytes 4194304 | tf_op jit(solution)/shard_map/convert_element_type | solution.py:27
  30.7 0.6 %fusion.23 = (f32[16,64]{1,0:T(8,128)S(1)}, f32[16,64,512]{2,1,0:T(8,128)S(1)}) fusion(f32[512]{0:T(512)S(1)} %add_multiply_fusion, f32[16,64,512]{2,1,0:T(8,128)S(1)} %reshape.37, bf16[64,16,24]{0,2,1:T(8,128)(2,1)S(1)} %bitcast.28, bf16[512,16,24]{0,2,1:T(8,128)(2,1)S(1)} %bitcast.25), kind=kOutput, calls=%fused_computation.33 | convolution fusion | flops 26737664 | bytes 4642816 | tf_op jit(solution)/shard_map/qhd,khd->hqk/dot_general | solution.py:25
  31.3 0.8 %fusion = f32[16,64]{1,0:T(8,128)S(1)} fusion(f32[16,64,512]{2,1,0:T(8,128)S(1)} %get-tuple-element.6, f32[16,64]{1,0:T(8,128)S(1)} %get-tuple-element.5), kind=kLoop, calls=%fused_computation.3 | loop fusion | flops 1047552 | bytes 2105344 | tf_op jit(solution)/shard_map/reduce_sum | solution.py:30
  32.1 0.0 copy-start.4
  32.1 0.5 %fusion.2 = f32[64,16,24]{0,2,1:T(8,128)S(1)} fusion(bf16[512,16,24]{0,2,1:T(8,128)(2,1)S(1)} %bitcast.26, f32[16,64,512]{2,1,0:T(8,128)S(1)} %get-tuple-element.6, f32[16,64]{1,0:T(8,128)S(1)} %get-tuple-element.5, f32[64,16]{0,1:T(8,128)S(1)} %bitcast.29), kind=kOutput, calls=%fused_computation.8 | convolution fusion | flops 26238976 | bytes 2596864 | tf_op jit(solution)/shard_map/hqk,khd->qhd/dot_general | solution.py:31
  32.6 0.1 copy.33
  32.7 0.9 %fusion.16 = bf16[64,384]{1,0:T(8,128)(2,1)S(1)} fusion(f32[64,384]{1,0:T(8,128)S(1)} %copy.33, f32[256,384]{1,0:T(8,128)} %fusion.21, s32[]{:T(128)S(6)} %select_n.8), kind=kLoop, calls=%fused_computation.26 | loop fusion | flops 122880 | bytes 245764 | tf_op jit(solution)/shard_map/convert_element_type | solution.py:71
  33.7 5.6 %all_gather.11 = bf16[256,384]{1,0:T(8,128)(2,1)S(1)} all-gather(bf16[64,384]{1,0:T(8,128)(2,1)S(1)} %fusion.16), channel_id=1, replica_groups=mesh['sample'=4,'row'=2,'col'=4] {'col'}, dimensions={0}, use_global_device_ids=true | all-gather | bytes 245760 | tf_op jit(solution)/shard_map/all_gather | solution.py:72
  39.3 0.0 copy-done.4
  39.3 0.8 %convolution_add_fusion = f32[256,96]{0,1:T(8,128)} fusion(bf16[256,384]{1,0:T(8,128)(2,1)S(1)} %all_gather.11, bf16[384,96]{0,1:T(8,128)(2,1)S(1)} %copy-done.4, bf16[256,96]{0,1:T(8,128)(2,1)S(1)} %copy.34), kind=kOutput, calls=%fused_computation.9 | convolution fusion | flops 18923520 | bytes 417792 | tf_op jit(solution)/shard_map/dot_general | solution.py:73
  (4 shorter events, 0.0 us)
Async XLA Ops:
  0.0 7.7 %copy-start = (bf16[384,384]{1,0:T(8,128)(2,1)S(1)}, bf16[384,384]{1,0:T(8,128)(2,1)}, u32[]{:S(2)}) copy-start(bf16[384,384]{1,0:T(8,128)(2,1)} %param.17) | copy-start | bytes 884740
  0.0 7.3 %copy-start.1 = (bf16[256,384]{1,0:T(8,128)(2,1)S(1)}, bf16[256,384]{1,0:T(8,128)(2,1)}, u32[]{:S(2)}) copy-start(bf16[256,384]{1,0:T(8,128)(2,1)} %param.10) | copy-start | bytes 589828
  0.0 7.7 %copy-start.5 = (f32[384]{0:T(512)S(1)}, f32[384]{0:T(512)}, u32[]{:S(2)}) copy-start(f32[384]{0:T(512)} %param.13) | copy-start | bytes 4612
  3.0 5.1 %copy-start.2 = (bf16[384,384]{1,0:T(8,128)(2,1)S(1)}, bf16[384,384]{1,0:T(8,128)(2,1)}, u32[]{:S(2)}) copy-start(bf16[384,384]{1,0:T(8,128)(2,1)} %param.14) | copy-start | bytes 884740
  3.0 5.5 %copy-start.8 = (bf16[384,384]{1,0:T(8,128)(2,1)S(1)}, bf16[384,384]{1,0:T(8,128)(2,1)}, u32[]{:S(2)}) copy-start(bf16[384,384]{1,0:T(8,128)(2,1)} %param.16) | copy-start | bytes 884740
  3.0 5.8 %copy-start.6 = (f32[384]{0:T(512)S(1)}, f32[384]{0:T(512)}, u32[]{:S(2)}) copy-start(f32[384]{0:T(512)} %param.15) | copy-start | bytes 4612
  3.0 23.5 %all-to-all-start = ((bf16[16,256,128]{2,0,1:T(8,128)(2,1)}), bf16[16,256,128]{2,0,1:T(8,128)(2,1)S(1)}, u32[]{:S(2)}, u32[]{:S(2)}) async-start(bf16[16,256,128]{2,0,1:T(8,128)(2,1)} %copy.31), calls=%async_computation | async-start | bytes 2097152 | tf_op jit(solution)/shard_map/all_to_all | solution.py:65
  8.4 17.0 %copy-start.7 = (s32[512]{0:T(512)S(1)}, s32[512]{0:T(512)}, u32[]{:S(2)}) copy-start(s32[512]{0:T(512)} %param.12) | copy-start | bytes 6148
  8.4 17.0 %copy-start.3 = (bf16[384,384]{1,0:T(8,128)(2,1)S(1)}, bf16[384,384]{1,0:T(8,128)(2,1)}, u32[]{:S(2)}) copy-start(bf16[384,384]{1,0:T(8,128)(2,1)} %param.18) | copy-start | bytes 884740
  32.1 7.2 %copy-start.4 = (bf16[384,96]{0,1:T(8,128)(2,1)S(1)}, bf16[384,96]{0,1:T(8,128)(2,1)}, u32[]{:S(2)}) copy-start(bf16[384,96]{0,1:T(8,128)(2,1)} %param.19) | copy-start | bytes 221188
where the time goes:
time: 40.4 us; the launch traced here: 40.1 us
  blocking collectives  21.4 us (53%)
  local copies, waits for them, and re-layouts  8.06 us (20%)
  starting transfers between devices  4.38 us (11%)
  matrix products  4.02 us (10%)
  other arithmetic  2.06 us (5%)
    all_gather x1, blocking collectives, on_device(): lax.all_gather(value_local, 'row', axis=0, tiled=True)  8.47 us
    all_gather x1, blocking collectives, on_device(): lax.all_gather(key_local, 'row', axis=0, tiled=True)  7.34 us
    all_gather x1, blocking collectives, on_device(): gated_all = lax.all_gather(gated_part, 'col', axis=0, tiled=True)  5.6 us
    all_to_all x1, starting transfers between devices, on_device(): lax.all_to_all(pair_bias, 'col', split_axis=1, concat_axis=2, tiled=True)  4.38 us
    convert_element_type x2, local copies, waits for them, and re-layouts, attend(): logits = logits + bias_block.astype(jnp.float32) + mask_term[None, None, :]  4.25 us
    unnamed x20, local copies, waits for them, and re-layouts  3.08 us
    dot_general x1, matrix products, on_device(): jnp.dot(normed, w_gate, preferred_element_type=jnp.float32)  1.09 us
    convert_element_type x1, other arithmetic, on_device(): gated_part = (gate_part * attended).astype(jnp.bfloat16)  0.94 us
  transfers between devices with their start and end apart: 1, of which 0 were waited for; matrix products, arithmetic and copies ran while one was open for 8% of the time, Pallas kernels for 0%

commit v1 on v0

--- a/solution.py
+++ b/solution.py
@@ -62,7 +62,10 @@
     )
     sub_rows = tok_rows // col_total
     query_start = col_pos * sub_rows
-    bias_panel = lax.all_to_all(pair_bias, "col", split_axis=1, concat_axis=2, tiled=True)
+    peers = lax.axis_size("col")
+    blocks = jnp.stack(jnp.split(pair_bias, peers, axis=1), axis=0)
+    blocks = lax.all_to_all(blocks, "col", split_axis=0, concat_axis=0)
+    bias_panel = jnp.concatenate(blocks, axis=2)
     key_rows, value_rows = (key_all, value_all)
     query_part = lax.dynamic_slice_in_dim(query, query_start, sub_rows, 0)
     gate_part = lax.dynamic_slice_in_dim(gate_act, query_start, sub_rows, 0)

time: 40.4 us -> 34 us (0.84)
  local copies, waits for them, and re-layouts: 8.06 us -> 2.17 us
  matrix products: 4.02 us -> 3.26 us
    convert_element_type x2 -> x0, local copies, waits for them, and re-layouts: 4.25 us -> none  [attend(): logits = logits + bias_block.astype(jnp.float32) + mask_term[None, None, :]]
    unnamed x20 -> x19, local copies, waits for them, and re-layouts: 3.08 us -> 0.15 us
    another operation x0 -> x1, local copies, waits for them, and re-layouts: none -> 1.31 us  [on_device(): blocks = jnp.stack(jnp.split(pair_bias, peers, axis=1), axis=0)]
    all_gather x1, blocking collectives: 7.34 us -> 8.48 us  [on_device(): lax.all_gather(key_local, 'row', axis=0, tiled=True)]
    all_gather x1, blocking collectives: 8.47 us -> 7.35 us  [on_device(): lax.all_gather(value_local, 'row', axis=0, tiled=True)]
    another operation x0 -> x1, other arithmetic: none -> 1.11 us  [on_device(): blocks = jnp.stack(jnp.split(pair_bias, peers, axis=1), axis=0)]
    convert_element_type x1, other arithmetic: 0.94 us -> 0.04 us  [on_device(): gated_part = (gate_part * attended).astype(jnp.bfloat16)]
    dot_general x1, matrix products: 1.09 us -> 0.33 us  [on_device(): jnp.dot(normed, w_gate, preferred_element_type=jnp.float32)]
  transfers between devices with their start and end apart: 1 -> 1, of which waited for: 0 -> 0; matrix products, arithmetic and copies ran while one was open for 8% -> 7% of each run, Pallas kernels for 0% -> 0%
where the time goes in v1:
time: 34 us; the launch traced here: 33.7 us
  blocking collectives  21.4 us (63%)
  starting transfers between devices  4.37 us (13%)
  matrix products  3.26 us (10%)
  other arithmetic  2.27 us (7%)
  local copies, waits for them, and re-layouts  2.17 us (6%)
    all_gather x1, blocking collectives, on_device(): lax.all_gather(key_local, 'row', axis=0, tiled=True)  8.48 us
    all_gather x1, blocking collectives, on_device(): lax.all_gather(value_local, 'row', axis=0, tiled=True)  7.35 us
    all_gather x1, blocking collectives, on_device(): gated_all = lax.all_gather(gated_part, 'col', axis=0, tiled=True)  5.6 us
    all_to_all x1, starting transfers between devices, on_device(): blocks = lax.all_to_all(blocks, 'col', split_axis=0, concat_axis=0)  4.37 us
    another operation x1, local copies, waits for them, and re-layouts, on_device(): blocks = jnp.stack(jnp.split(pair_bias, peers, axis=1), axis=0)  1.31 us
    another operation x1, other arithmetic, on_device(): blocks = jnp.stack(jnp.split(pair_bias, peers, axis=1), axis=0)  1.11 us
    dot_general x1, matrix products, on_device(): jnp.dot(gated_all, w_out, preferred_element_type=jnp.float32)  0.85 us
    reduce_sum x1, other arithmetic, attend(): row_total = jnp.sum(exp_scores, axis=2)  0.78 us
  transfers between devices with their start and end apart: 1, of which 0 were waited for; matrix products, arithmetic and copies ran while one was open for 7% of the time, Pallas kernels for 0%

profile of v1, /device:TPU:0, one launch (start us, length us, event | category | flops | bytes accessed | tf_op | source)
XLA Modules:
  0.0 33.7 jit_solution(9422909382869816491)
XLA Ops:
  0.0 0.0 copy-start
  0.0 1.3 %slice_bitcast_fusion.3 = (bf16[1,16,64,128]{3,2,1,0:T(8,128)(2,1)S(1)}, bf16[1,16,64,128]{3,2,1,0:T(8,128)(2,1)S(1)}, bf16[1,16,64,128]{3,2,1,0:T(8,128)(2,1)S(1)}, bf16[1,16,64,128]{3,2,1,0:T(8,128)(2,1)S(1)}) fusion(bf16[16,256,128]{2,1,0:T(8,128)(2,1)} %param.11), kind=kLoop, calls=%fused_computation.23 | loop fusion | bytes 2097152 | tf_op jit(solution)/shard_map/stack | solution.py:66
  1.3 0.0 copy-start.1
  1.3 0.0 copy-start.4
  1.3 1.1 %pad_maximum_fusion = bf16[4,16,64,128]{3,2,1,0:T(8,128)(2,1)} fusion(bf16[1,16,64,128]{3,2,1,0:T(8,128)(2,1)S(1)} %get-tuple-element.7, bf16[1,16,64,128]{3,2,1,0:T(8,128)(2,1)S(1)} %get-tuple-element.8, bf16[1,16,64,128]{3,2,1,0:T(8,128)(2,1)S(1)} %get-tuple-element.6, bf16[1,16,64,128]{3,2,1,0:T(8,128)(2,1)S(1)} %get-tuple-element.5), kind=kLoop, calls=%fused_computation.11 | loop fusion | flops 1572864 | bytes 2097152 | tf_op jit(solution)/shard_map/stack | solution.py:66
  2.4 0.0 copy-start.7
  2.4 0.0 copy-start.8
  2.5 0.0 copy-start.5
  2.5 4.4 %all-to-all-start = ((bf16[4,16,64,128]{3,2,1,0:T(8,128)(2,1)}), bf16[4,16,64,128]{3,2,1,0:T(8,128)(2,1)S(1)}, u32[]{:S(2)}, u32[]{:S(2)}) async-start(bf16[4,16,64,128]{3,2,1,0:T(8,128)(2,1)} %pad_maximum_fusion), calls=%async_computation | async-start | bytes 2097152 | tf_op jit(solution)/shard_map/all_to_all | solution.py:67
  6.8 0.0 copy-done.1
  6.8 0.1 convert_reduce_fusion
  7.0 0.2 fusion.8
  7.2 0.0 copy-done
  7.2 0.0 copy-done.4
  7.2 0.3 fusion.19
  7.5 0.0 copy-done.7
  7.5 0.3 convolution_convert_fusion
  7.9 0.0 copy-done.8
  7.9 0.0 copy-start.6
  7.9 0.0 copy-start.2
  7.9 0.3 convolution_convert_fusion.1
  8.2 0.0 copy-done.5
  8.3 0.1 copy.28
  8.4 8.5 %all_gather.10 = bf16[512,384]{1,0:T(8,128)(2,1)S(1)} all-gather(bf16[256,384]{1,0:T(8,128)(2,1)S(1)} %convolution_convert_fusion), channel_id=1, replica_groups=mesh['sample'=4,'row'=2,'col'=4] {'row'}, dimensions={0}, use_global_device_ids=true | all-gather | bytes 589824 | tf_op jit(solution)/shard_map/all_gather | solution.py:60
  16.9 0.2 copy.29
  17.1 7.4 %all_gather.9 = bf16[512,384]{1,0:T(8,128)(2,1)S(1)} all-gather(bf16[256,384]{1,0:T(8,128)(2,1)S(1)} %convolution_convert_fusion.1), channel_id=1, replica_groups=mesh['sample'=4,'row'=2,'col'=4] {'row'}, dimensions={0}, use_global_device_ids=true | all-gather | bytes 589824 | tf_op jit(solution)/shard_map/all_gather | solution.py:61
  24.4 0.2 copy.27
  24.6 0.1 constant_dynamic-slice_fusion
  24.7 0.1 copy.32
  24.8 0.0 copy-done.6
  24.9 0.0 copy-done.2
  24.9 0.3 fusion.22
  25.2 0.0 all-to-all-done
  25.2 0.6 %fusion.24 = (f32[16,64]{1,0:T(8,128)S(1)}, f32[16,64,512]{2,1,0:T(8,128)S(1)}) fusion(f32[512]{0:T(512)S(1)} %add_multiply_fusion, bf16[64,16,24]{0,2,1:T(8,128)(2,1)S(1)} %bitcast.37, bf16[512,16,24]{0,2,1:T(8,128)(2,1)S(1)} %bitcast.34, bf16[4,16,64,128]{3,2,1,0:T(8,128)(2,1)S(1)} %all-to-all-done), kind=kOutput, calls=%fused_computation.39 | convolution fusion | flops 27261952 | bytes 3594240 | tf_op jit(solution)/shard_map/qhd,khd->hqk/dot_general | solution.py:25
  25.8 0.8 %fusion.1 = f32[16,64]{1,0:T(8,128)S(1)} fusion(f32[16,64,512]{2,1,0:T(8,128)S(1)} %get-tuple-element.10, f32[16,64]{1,0:T(8,128)S(1)} %get-tuple-element.9), kind=kLoop, calls=%fused_computation.4 | loop fusion | flops 1047552 | bytes 2105344 | tf_op jit(solution)/shard_map/reduce_sum | solution.py:30
  26.6 0.0 copy-start.3
  26.6 0.5 %fusion.3 = f32[64,16,24]{0,2,1:T(8,128)S(1)} fusion(bf16[512,16,24]{0,2,1:T(8,128)(2,1)S(1)} %bitcast.35, f32[16,64,512]{2,1,0:T(8,128)S(1)} %get-tuple-element.10, f32[16,64]{1,0:T(8,128)S(1)} %get-tuple-element.9, f32[64,16]{0,1:T(8,128)S(1)} %bitcast.38), kind=kOutput, calls=%fused_computation.9 | convolution fusion | flops 26238976 | bytes 2596864 | tf_op jit(solution)/shard_map/hqk,khd->qhd/dot_general | solution.py:31
  27.1 0.1 copy.31
  27.3 5.6 %all_gather.11 = bf16[256,384]{1,0:T(8,128)(2,1)S(1)} all-gather(bf16[64,384]{1,0:T(8,128)(2,1)S(1)} %fusion.17), channel_id=1, replica_groups=mesh['sample'=4,'row'=2,'col'=4] {'col'}, dimensions={0}, use_global_device_ids=true | all-gather | bytes 245760 | tf_op jit(solution)/shard_map/all_gather | solution.py:75
  32.9 0.0 copy-done.3
  32.9 0.9 %convolution_add_fusion = f32[256,96]{0,1:T(8,128)} fusion(bf16[256,384]{1,0:T(8,128)(2,1)S(1)} %all_gather.11, bf16[384,96]{0,1:T(8,128)(2,1)S(1)} %copy-done.3, bf16[256,96]{0,1:T(8,128)(2,1)S(1)} %copy.32), kind=kOutput, calls=%fused_computation.10 | convolution fusion | flops 18923520 | bytes 417792 | tf_op jit(solution)/shard_map/dot_general | solution.py:76
  (5 shorter events, 0.1 us)
Async XLA Ops:
  0.0 7.2 %copy-start = (bf16[384,384]{1,0:T(8,128)(2,1)S(1)}, bf16[384,384]{1,0:T(8,128)(2,1)}, u32[]{:S(2)}) copy-start(bf16[384,384]{1,0:T(8,128)(2,1)} %param.14) | copy-start | bytes 884740
  1.3 5.5 %copy-start.1 = (bf16[256,384]{1,0:T(8,128)(2,1)S(1)}, bf16[256,384]{1,0:T(8,128)(2,1)}, u32[]{:S(2)}) copy-start(bf16[256,384]{1,0:T(8,128)(2,1)} %param.10) | copy-start | bytes 589828
  1.3 5.9 %copy-start.4 = (f32[384]{0:T(512)S(1)}, f32[384]{0:T(512)}, u32[]{:S(2)}) copy-start(f32[384]{0:T(512)} %param.13) | copy-start | bytes 4612
  2.4 5.1 %copy-start.7 = (bf16[384,384]{1,0:T(8,128)(2,1)S(1)}, bf16[384,384]{1,0:T(8,128)(2,1)}, u32[]{:S(2)}) copy-start(bf16[384,384]{1,0:T(8,128)(2,1)} %param.16) | copy-start | bytes 884740
  2.4 5.4 %copy-start.8 = (bf16[384,384]{1,0:T(8,128)(2,1)S(1)}, bf16[384,384]{1,0:T(8,128)(2,1)}, u32[]{:S(2)}) copy-start(bf16[384,384]{1,0:T(8,128)(2,1)} %param.17) | copy-start | bytes 884740
  2.5 5.8 %copy-start.5 = (f32[384]{0:T(512)S(1)}, f32[384]{0:T(512)}, u32[]{:S(2)}) copy-start(f32[384]{0:T(512)} %param.15) | copy-start | bytes 4612
  2.5 22.8 %all-to-all-start = ((bf16[4,16,64,128]{3,2,1,0:T(8,128)(2,1)}), bf16[4,16,64,128]{3,2,1,0:T(8,128)(2,1)S(1)}, u32[]{:S(2)}, u32[]{:S(2)}) async-start(bf16[4,16,64,128]{3,2,1,0:T(8,128)(2,1)} %pad_maximum_fusion), calls=%async_computation | async-start | bytes 2097152 | tf_op jit(solution)/shard_map/all_to_all | solution.py:67
  7.9 17.0 %copy-start.6 = (s32[512]{0:T(512)S(1)}, s32[512]{0:T(512)}, u32[]{:S(2)}) copy-start(s32[512]{0:T(512)} %param.12) | copy-start | bytes 6148
  7.9 17.0 %copy-start.2 = (bf16[384,384]{1,0:T(8,128)(2,1)S(1)}, bf16[384,384]{1,0:T(8,128)(2,1)}, u32[]{:S(2)}) copy-start(bf16[384,384]{1,0:T(8,128)(2,1)} %param.18) | copy-start | bytes 884740
  26.6 6.3 %copy-start.3 = (bf16[384,96]{0,1:T(8,128)(2,1)S(1)}, bf16[384,96]{0,1:T(8,128)(2,1)}, u32[]{:S(2)}) copy-start(bf16[384,96]{0,1:T(8,128)(2,1)} %param.19) | copy-start | bytes 221188
